TPU v7x, 32 devices: a whole 2x2x4 slice. The times are simulated.
32 devices in a mesh: blk: 8 (over z, x), sub: 4 (over y, core).
Axes of the slice: x: 2, y: 2, z: 4, core: 2. Of those that a mesh axis runs over, the one named last changes fastest.
Arguments:
- features: bfloat16 [12288, 768], P(('blk', 'sub')), may hold values from -6 to 6
- scales: bfloat16 [12288], P('blk'), may hold values from 0.5 to 4
- neighbor_lists: int32 [9, 16, 12288], P(None, None, 'blk'), may hold values from 0 to 1535, as said below
- eigen_block: float32 [64, 12288], P(None, ('blk', 'sub')), may hold values from -6 to 6
Outputs:
- embedding: float32 [64, 12288], P(None, ('blk', 'sub'))
Inputs may be any that keep to these rules, and one draw needn't show every extreme that they name: For each j and point p, the 16 entries neighbor_lists[j, :, p] are distinct positions within the row block that lies j - 4 blocks before p's block, counted cyclically.
All inputs are finite; a program needn't handle non-finite values.
Results may differ from a plain program's by a relative error of at most 0.0039.
Values may be sent and summed in bfloat16 or wider, within the bound.
A program may use at most 128 MiB of HBM per device.

v0:
```python
import math
import jax
import jax.numpy as jnp
from jax import lax
from jax.sharding import PartitionSpec as P

F = 768


def as_sent(value):
    return jax.tree.map(lambda a: a.astype(jnp.bfloat16) if a.dtype == jnp.float32 else a, value)


def shifted(value, axis, steps):
    count = lax.axis_size(axis)
    pairs = [(source, (source + steps) % count) for source in range(count)]
    return lax.ppermute(value, axis, pairs)


def pair_weights(
    block_feats, block_norms, block_scales, lists_here, positions, moving_feats, moving_scales
):
    inner = lax.dot_general(
        block_feats, moving_feats, (((1,), (1,)), ((), ())), preferred_element_type=jnp.float32
    )
    moving_norms = jnp.sum(jnp.square(moving_feats.astype(jnp.float32)), axis=1)
    distance = block_norms[:, None] + moving_norms[None, :] - 2.0 * inner
    spread = F * block_scales[:, None] * moving_scales.astype(jnp.float32)[None, :]
    affinity = jnp.exp(-distance / spread)
    listed = jnp.sum(
        (lists_here[:, :, None] == positions[None, None, :]).astype(jnp.float32), axis=0
    )
    return affinity * listed


def band_sweep(payload, work, half):
    row_total, col_total = work(half, payload)
    for heading in (1, -1):
        pieces = payload
        owed = []
        for travel in range(1, half + 1):
            pieces = jax.tree.map(
                lambda part, own: part.astype(own.dtype),
                shifted(as_sent(pieces), "blk", heading),
                pieces,
            )
            row_term, col_term = work(heading * travel + half, pieces)
            row_total = row_total + row_term
            owed.append(col_term)
        carried = jnp.zeros_like(owed[0])
        for travel in range(half - 1, -1, -1):
            carried = shifted(carried + owed[travel], "blk", -heading)
        col_total = col_total + carried
    return (row_total, col_total)


def to_owners(terms):
    return lax.psum_scatter(terms, "sub", scatter_dimension=1, tiled=True)


def local(features, scales, neighbor_lists, eigen_block):
    rows_dev = features.shape[0]
    sub_index = lax.axis_index("sub")
    half = (neighbor_lists.shape[0] - 1) // 2
    block_feats = lax.all_gather(features, "sub", axis=0, tiled=True)
    block_norms = jnp.sum(jnp.square(block_feats.astype(jnp.float32)), axis=1)
    block_scales = scales.astype(jnp.float32)
    own_scales = lax.dynamic_slice_in_dim(scales, sub_index * rows_dev, rows_dev)
    positions = sub_index * rows_dev + jnp.arange(rows_dev, dtype=jnp.int32)

    def weights(shift_index, pieces):
        return pair_weights(
            block_feats,
            block_norms,
            block_scales,
            neighbor_lists[shift_index],
            positions,
            pieces[0],
            pieces[1],
        )

    def degree_work(shift_index, pieces):
        tile = weights(shift_index, pieces)
        return (jnp.sum(tile, axis=1)[None, :], jnp.sum(tile, axis=0)[None, :])

    row_deg, col_deg = band_sweep((features, own_scales), degree_work, half)
    degree = 1.0 + 0.5 * (to_owners(row_deg) + col_deg)
    inv_root = lax.rsqrt(degree)
    scaled = eigen_block * inv_root
    scaled_low = scaled.astype(jnp.bfloat16)
    block_eigen = lax.all_gather(scaled_low, "sub", axis=1, tiled=True)

    def product_work(shift_index, pieces):
        tile = weights(shift_index, pieces).astype(jnp.bfloat16)
        moving_eigen = pieces[2]
        row_term = lax.dot_general(
            moving_eigen, tile, (((1,), (1,)), ((), ())), preferred_element_type=jnp.float32
        )
        col_term = jnp.dot(block_eigen, tile, preferred_element_type=jnp.float32)
        return (row_term, col_term)

    product_payload = (features, own_scales, scaled_low)
    row_side, col_side = band_sweep(product_payload, product_work, half)
    mixed = inv_root * (scaled + 0.5 * (to_owners(row_side) + col_side))
    partial_gram = jnp.dot(
        mixed, mixed.T, precision=lax.Precision.HIGHEST, preferred_element_type=jnp.float32
    )
    gram = lax.psum(partial_gram, ("blk", "sub"))
    lower = jnp.linalg.cholesky(gram)
    total_rows = rows_dev * lax.axis_size("blk") * lax.axis_size("sub")
    return math.sqrt(total_rows) * jax.scipy.linalg.solve_triangular(lower, mixed, lower=True)


def solution(mesh):
    placed = (P(("blk", "sub"), None), P("blk"), P(None, None, "blk"), P(None, ("blk", "sub")))
    return jax.shard_map(
        local, mesh=mesh, in_specs=placed, out_specs=P(None, ("blk", "sub")), check_vma=False
    )
```

profile of v0, /device:TPU:10, one launch (start us, length us, event | category | flops | bytes accessed | tf_op | source)
XLA Modules:
  0.0 344.4 jit_solution(11951891037983374221)
XLA Ops:
  7.3 1.6 collective-permute-start
  15.0 20.4 %collective-permute-done.1 = bf16[384]{0:T(512)(128)(2,1)S(1)} collective-permute-done((bf16[384]{0:T(512)(128)(2,1)S(1)}, bf16[384]{0:T(512)(128)(2,1)S(1)}, u32[]{:S(2)}, u32[]{:S(2)}) %collective-permute-start.1) | collective-permute-done | bytes 800 | tf_op jit(solution)/shard_map/ppermute | solution.py:17
  37.4 1.5 collective-permute-start.2
  39.4 44.8 %convert_reduce_fusion.7 = (f32[1536,384]{1,0:T(8,128)}, f32[1536,384]{1,0:T(8,128)}, f32[1536,384]{1,0:T(8,128)}, f32[1536,384]{1,0:T(8,128)}, f32[1536,384]{1,...) fusion(s32[16,1536]{1,0:T(8,128)S(1)} %get-tuple-element.40, ...), kind=kLoop, calls=%fused_computation.7 | loop fusion | flops 249495552 | bytes 22119936 | tf_op jit(solution)/shard_map/reduce_sum | solution.py:30
  84.3 2.4 collective-permute-start.5
  86.7 2.9 collective-permute-start.4
  89.6 1.5 collective-permute-start.7
  91.7 1.8 collective-permute-start.12
  97.1 15.2 %collective-permute-done.7 = bf16[384]{0:T(512)(128)(2,1)S(1)} collective-permute-done((bf16[384]{0:T(512)(128)(2,1)S(1)}, bf16[384]{0:T(512)(128)(2,1)S(1)}, u32[]{:S(2)}, u32[]{:S(2)}) %collective-permute-start.7) | collective-permute-done | bytes 800 | tf_op jit(solution)/shard_map/ppermute | solution.py:17
  115.9 1.5 collective-permute-start.14
  119.7 6.8 %collective-permute-done.6 = bf16[384,768]{1,0:T(8,128)(2,1)S(1)} collective-permute-done((bf16[384,768]{1,0:T(8,128)(2,1)S(1)}, bf16[384,768]{1,0:T(8,128)(2,1)S(1)}, u32[]{:S(2)}, u32[]{:S(2)}) %collective-permute-start.6) | collective-permute-done | bytes 589856 | tf_op jit(solution)/shard_map/ppermute | solution.py:17
  127.3 14.6 %collective-permute-done.14 = bf16[384,768]{1,0:T(8,128)(2,1)S(1)} collective-permute-done((bf16[384,768]{1,0:T(8,128)(2,1)S(1)}, bf16[384,768]{1,0:T(8,128)(2,1)S(1)}, u32[]{:S(2)}, u32[]{:S(2)}) %collective-permute-start.14) | collective-permute-done | bytes 589856 | tf_op jit(solution)/shard_map/ppermute | solution.py:17
  143.5 2.3 multiply_reduce_fusion
  145.9 4.2 %fusion.40 = (f32[384]{0:T(512)S(1)}, f32[1536]{0:T(1024)S(1)}, bf16[1536,384]{1,0:T(8,128)(2,1)S(1)}) fusion(f32[1536,384]{1,0:T(8,128)} %get-tuple-element.26, f32[384]{0:T(512)} %convert_element_type.159, f32[1536]{0:T(1024)S(1)} %convert_multiply_fusion, bf16[1536,768]{1,0:T(8,128)(2,1)S(1)} %copy-done.8, bf16[384,768]{1,0:T(8,128)(2,1)} %copy-done.26, ...), kind=kOutput, calls=%fused_computation.114 | convolution fusion | flops 911865984 | bytes 6511104 | tf_op jit(solution)/shard_map/dot_general | solution.py:23
  150.7 2.0 collective-permute-start.16
  152.7 3.4 fusion.44
  157.7 4.0 %fusion.39 = (f32[384]{0:T(512)}, f32[1536]{0:T(1024)S(1)}, bf16[1536,384]{1,0:T(8,128)(2,1)}) fusion(f32[1536,384]{1,0:T(8,128)S(1)} %copy-done.16, f32[384]{0:T(512)S(1)} %copy-done.41, f32[1536]{0:T(1024)S(1)} %convert_multiply_fusion, bf16[1536,768]{1,0:T(8,128)(2,1)S(1)} %copy-done.8, bf16[384,768]{1,0:T(8,128)(2,1)S(1)} %copy-done.23, ...), kind=kOutput, calls=%fused_computation.113 | convolution fusion | flops 911865984 | bytes 6511104 | tf_op jit(solution)/shard_map/dot_general | solution.py:23
  161.7 4.0 %fusion.38 = (f32[384]{0:T(512)}, f32[1536]{0:T(1024)S(1)}, bf16[1536,384]{1,0:T(8,128)(2,1)}) fusion(f32[1536,384]{1,0:T(8,128)S(1)} %copy-done.15, f32[384]{0:T(512)S(1)} %copy-done.40, f32[1536]{0:T(1024)S(1)} %convert_multiply_fusion, bf16[1536,768]{1,0:T(8,128)(2,1)S(1)} %copy-done.8, bf16[384,768]{1,0:T(8,128)(2,1)S(1)} %copy-done.19, ...), kind=kOutput, calls=%fused_computation.112 | convolution fusion | flops 911865984 | bytes 6511104 | tf_op jit(solution)/shard_map/dot_general | solution.py:23
  165.7 3.9 %fusion.37 = (f32[384]{0:T(512)}, f32[1536]{0:T(1024)S(1)}, bf16[1536,384]{1,0:T(8,128)(2,1)}) fusion(f32[1536,384]{1,0:T(8,128)S(1)} %copy-done.14, f32[384]{0:T(512)S(1)} %copy-done.38, f32[1536]{0:T(1024)S(1)} %convert_multiply_fusion, bf16[1536,768]{1,0:T(8,128)(2,1)S(1)} %copy-done.8, bf16[384,768]{1,0:T(8,128)(2,1)S(1)} %collective-permute-done, ...), kind=kOutput, calls=%fused_computation.111 | convolution fusion | flops 911865984 | bytes 6511104 | tf_op jit(solution)/shard_map/dot_general | solution.py:23
  169.7 3.9 %fusion.43 = (f32[384]{0:T(512)}, f32[1536]{0:T(1024)S(1)}, bf16[1536,384]{1,0:T(8,128)(2,1)}) fusion(f32[1536,384]{1,0:T(8,128)S(1)} %copy-done.13, f32[384]{0:T(512)S(1)} %copy-done.39, f32[1536]{0:T(1024)S(1)} %convert_multiply_fusion, bf16[1536,768]{1,0:T(8,128)(2,1)S(1)} %copy-done.8, bf16[384,768]{1,0:T(8,128)(2,1)S(1)} %copy-done.21, ...), kind=kOutput, calls=%fused_computation.117 | convolution fusion | flops 911865984 | bytes 6511104 | tf_op jit(solution)/shard_map/dot_general | solution.py:23
  173.7 4.1 %fusion.42 = (f32[384]{0:T(512)}, f32[1536]{0:T(1024)S(1)}, bf16[1536,384]{1,0:T(8,128)(2,1)}) fusion(f32[1536,384]{1,0:T(8,128)S(1)} %copy-done.12, f32[384]{0:T(512)S(1)} %copy-done.37, f32[1536]{0:T(1024)S(1)} %convert_multiply_fusion, bf16[1536,768]{1,0:T(8,128)(2,1)S(1)} %copy-done.8, bf16[384,768]{1,0:T(8,128)(2,1)S(1)} %collective-permute-done.10, ...), kind=kOutput, calls=%fused_computation.116 | convolution fusion | flops 911865984 | bytes 6511104 | tf_op jit(solution)/shard_map/dot_general | solution.py:23
  177.7 3.4 fusion.41
  181.2 2.6 fusion.36
  185.8 5.4 %collective-permute-start.17 = (f32[1,384]{1,0:T(1,128)S(1)}, f32[1,384]{1,0:T(1,128)S(1)}, u32[]{:S(2)}, u32[]{:S(2)}) collective-permute-start(f32[1,384]{1,0:T(1,128)S(1)} %reshape_add_fusion.5), channel_id=1, source_target_pairs={{0,28},{4,0},{8,4},{12,8},{16,12},{20,16},{24,20},{28,24},{1,29},{... | collective-permute-start | bytes 4616 | tf_op jit(solution)/shard_map/ppermute | solution.py:17
  192.5 2.9 collective-permute-start.18
  197.0 2.9 collective-permute-start.19
  200.9 17.3 %reduce-scatter.7.cloned.1.call-done = f32[384,1]{1,0:T(8,128)} async-done(((f32[1536,1]{1,0:T(8,128)}), f32[384,1]{1,0:T(8,128)}) %reduce-scatter.7.cloned.1.call-update) | async-done | bytes 1552
  219.3 5.7 %all_gather.7 = bf16[64,1536]{1,0:T(8,128)(2,1)S(1)} all-gather(bf16[64,384]{1,0:T(8,128)(2,1)S(1)} %multiply_convert_fusion), channel_id=1, replica_groups=mesh['blk'=8,'sub'=4] {'sub'}, dimensions={1}, use_global_device_ids=true | all-gather | bytes 245760 | tf_op jit(solution)/shard_map/all_gather | solution.py:91
  227.1 1.6 fusion.26
  228.7 1.6 fusion.23
  230.6 1.5 collective-permute-start.32
  232.4 1.5 collective-permute-start.36
  234.5 1.5 collective-permute-start.25
  237.6 2.1 collective-permute-done.25
  242.6 1.6 collective-permute-start.33
  244.3 1.8 collective-permute-start.27
  247.4 1.9 collective-permute-done.27
  253.0 1.7 convolution_add_fusion.7
  255.6 1.6 fusion.11
  257.2 2.6 collective-permute-start.34
  261.6 2.7 collective-permute-done.34
  264.3 2.5 collective-permute-start.35
  267.7 1.7 collective-permute-start.39
  269.7 2.2 collective-permute-done.35
  273.0 7.3 %reduce-scatter.5.cloned.1.call-done = f32[64,384]{1,0:T(8,128)} async-done(((f32[64,1536]{1,0:T(8,128)}), f32[64,384]{1,0:T(8,128)}) %reduce-scatter.5.cloned.1.call-update) | async-done | bytes 98320 | tf_op jit(solution)/shard_map/reduce_scatter | solution.py:58
  281.5 43.3 %psum.7 = f32[64,64]{0,1:T(8,128)S(1)} all-reduce(f32[64,64]{0,1:T(8,128)S(1)} %fusion.46), channel_id=1, replica_groups=mesh['blk'=8,'sub'=4] {'blk','sub'}, use_global_device_ids=true, to_apply=%region_39.0 | all-reduce | flops 4096 | bytes 32768 | tf_op jit(solution)/shard_map/psum | solution.py:108
  324.8 5.8 %cholesky.16 = f32[64,64]{1,0:T(8,128)S(1)} custom-call(f32[64,64]{1,0:T(8,128)S(1)} %fusion.35), custom_call_target="Cholesky" | custom-call | tf_op jit(solution)/shard_map/jit(cholesky)/cholesky | solution.py:109
  332.0 4.9 %custom-call.7 = f32[1,64,64]{1,2,0:T(8,128)S(1)} custom-call(f32[1,64,64]{2,1,0:T(8,128)S(1)} %fusion.33), custom_call_target="InvertDiagBlocksLowerTriangular" | custom-call | tf_op jit(solution)/shard_map/jit(_solve_triangular)/triangular_solve | solution.py:111
  (218 shorter events, 51.8 us)
Async XLA Ops:
  6.5 136.9 %all-gather.2.cloned.1.call-start = ((), (), s32[]{:S(2)}) async-start(), calls=%async_computation.2 | async-start | bytes 2949120 | tf_op jit(solution)/shard_map/all_gather | solution.py:65
  7.3 210.9 %reduce-scatter.7.cloned.1.call-start = ((), (), s32[]{:S(2)}) async-start(), calls=%async_computation.4 | async-start | bytes 983040
  7.3 30.1 %collective-permute-start = (bf16[384,768]{1,0:T(8,128)(2,1)}, bf16[384,768]{1,0:T(8,128)(2,1)S(1)}, u32[]{:S(2)}, u32[]{:S(2)}) collective-permute-start(bf16[384,768]{1,0:T(8,128)(2,1)} %param.4), channel_id=1, source_target_pairs={{0,4},{4,8},{8,12},{12,16},{16,20},{20,24},{24,28},{28,0},{1,5},{5... | collective-permute-start | bytes 1769480 | tf_op jit(solution)/shard_map/ppermute | solution.py:17
  10.2 25.1 %collective-permute-start.1 = (bf16[384]{0:T(512)(128)(2,1)S(1)}, bf16[384]{0:T(512)(128)(2,1)S(1)}, u32[]{:S(2)}, u32[]{:S(2)}) collective-permute-start(bf16[384]{0:T(512)(128)(2,1)S(1)} %get-tuple-element.33), channel_id=1, source_target_pairs={{0,4},{4,8},{8,12},{12,16},{16,20},{20,24},{24,28},{28,0},{1,5},{5... | collective-permute-start | bytes 2312 | tf_op jit(solution)/shard_map/ppermute | solution.py:17
  11.7 24.2 %collective-permute-start.9 = (bf16[384]{0:T(512)(128)(2,1)S(1)}, bf16[384]{0:T(512)(128)(2,1)S(1)}, u32[]{:S(2)}, u32[]{:S(2)}) collective-permute-start(bf16[384]{0:T(512)(128)(2,1)S(1)} %get-tuple-element.33), channel_id=1, source_target_pairs={{0,28},{4,0},{8,4},{12,8},{16,12},{20,16},{24,20},{28,24},{1,29},{... | collective-permute-start | bytes 2312 | tf_op jit(solution)/shard_map/ppermute | solution.py:17
  12.3 26.6 %collective-permute-start.8 = (bf16[384,768]{1,0:T(8,128)(2,1)}, bf16[384,768]{1,0:T(8,128)(2,1)S(1)}, u32[]{:S(2)}, u32[]{:S(2)}) collective-permute-start(bf16[384,768]{1,0:T(8,128)(2,1)} %param.4), channel_id=1, source_target_pairs={{0,28},{4,0},{8,4},{12,8},{16,12},{20,16},{24,20},{28,24},{1,29},{... | collective-permute-start | bytes 1769480 | tf_op jit(solution)/shard_map/ppermute | solution.py:17
  35.4 48.9 %collective-permute-start.3 = (bf16[384]{0:T(512)(128)(2,1)S(1)}, bf16[384]{0:T(512)(128)(2,1)S(1)}, u32[]{:S(2)}, u32[]{:S(2)}) collective-permute-start(bf16[384]{0:T(512)(128)(2,1)S(1)} %collective-permute-done.1), channel_id=1, source_target_pairs={{0,4},{4,8},{8,12},{12,16},{16,20},{20,24},{24,28},{28,0},{1,5},{5... | collective-permute-start | bytes 2312 | tf_op jit(solution)/shard_map/ppermute | solution.py:17
  36.0 50.7 %collective-permute-start.11 = (bf16[384]{0:T(512)(128)(2,1)S(1)}, bf16[384]{0:T(512)(128)(2,1)S(1)}, u32[]{:S(2)}, u32[]{:S(2)}) collective-permute-start(bf16[384]{0:T(512)(128)(2,1)S(1)} %collective-permute-done.9), channel_id=1, source_target_pairs={{0,28},{4,0},{8,4},{12,8},{16,12},{20,16},{24,20},{28,24},{1,29},{... | collective-permute-start | bytes 2312 | tf_op jit(solution)/shard_map/ppermute | solution.py:17
  37.4 49.3 %collective-permute-start.2 = (bf16[384,768]{1,0:T(8,128)(2,1)S(1)}, bf16[384,768]{1,0:T(8,128)(2,1)S(1)}, u32[]{:S(2)}, u32[]{:S(2)}) collective-permute-start(bf16[384,768]{1,0:T(8,128)(2,1)S(1)} %collective-permute-done), channel_id=1, source_target_pairs={{0,4},{4,8},{8,12},{12,16},{16,20},{20,24},{24,28},{28,0},{1,5},{5... | collective-permute-start | bytes 1769480 | tf_op jit(solution)/shard_map/ppermute | solution.py:17
  38.9 52.8 %collective-permute-start.10 = (bf16[384,768]{1,0:T(8,128)(2,1)S(1)}, bf16[384,768]{1,0:T(8,128)(2,1)S(1)}, u32[]{:S(2)}, u32[]{:S(2)}) collective-permute-start(bf16[384,768]{1,0:T(8,128)(2,1)S(1)} %collective-permute-done.8), channel_id=1, source_target_pairs={{0,28},{4,0},{8,4},{12,8},{16,12},{20,16},{24,20},{28,24},{1,29},{... | collective-permute-start | bytes 1769480 | tf_op jit(solution)/shard_map/ppermute | solution.py:17
  39.4 50.2 %copy-start.28 = (bf16[1536]{0:T(1024)(128)(2,1)S(1)}, bf16[1536]{0:T(1024)(128)(2,1)}, u32[]{:S(2)}) copy-start(bf16[1536]{0:T(1024)(128)(2,1)} %param.5) | copy-start | bytes 9220
  39.4 54.0 %copy-start.9 = (bf16[384,768]{1,0:T(8,128)(2,1)S(1)}, bf16[384,768]{1,0:T(8,128)(2,1)}, u32[]{:S(2)}) copy-start(bf16[384,768]{1,0:T(8,128)(2,1)} %param.4) | copy-start | bytes 1769476
  84.3 5.4 %collective-permute-start.5 = (bf16[384]{0:T(512)(128)(2,1)S(1)}, bf16[384]{0:T(512)(128)(2,1)S(1)}, u32[]{:S(2)}, u32[]{:S(2)}) collective-permute-start(bf16[384]{0:T(512)(128)(2,1)S(1)} %collective-permute-done.3), channel_id=1, source_target_pairs={{0,4},{4,8},{8,12},{12,16},{16,20},{20,24},{24,28},{28,0},{1,5},{5... | collective-permute-start | bytes 2312 | tf_op jit(solution)/shard_map/ppermute | solution.py:17
  86.7 4.5 %collective-permute-start.13 = (bf16[384]{0:T(512)(128)(2,1)S(1)}, bf16[384]{0:T(512)(128)(2,1)S(1)}, u32[]{:S(2)}, u32[]{:S(2)}) collective-permute-start(bf16[384]{0:T(512)(128)(2,1)S(1)} %collective-permute-done.11), channel_id=1, source_target_pairs={{0,28},{4,0},{8,4},{12,8},{16,12},{20,16},{24,20},{28,24},{1,29},{... | collective-permute-start | bytes 2312 | tf_op jit(solution)/shard_map/ppermute | solution.py:17
  86.7 40.6 %copy-start.18 = (bf16[384,768]{1,0:T(8,128)(2,1)}, bf16[384,768]{1,0:T(8,128)(2,1)S(1)}, u32[]{:S(2)}) copy-start(bf16[384,768]{1,0:T(8,128)(2,1)S(1)} %collective-permute-done.2) | copy-start | bytes 1769476
  86.7 27.8 %collective-permute-start.4 = (bf16[384,768]{1,0:T(8,128)(2,1)S(1)}, bf16[384,768]{1,0:T(8,128)(2,1)S(1)}, u32[]{:S(2)}, u32[]{:S(2)}) collective-permute-start(bf16[384,768]{1,0:T(8,128)(2,1)S(1)} %collective-permute-done.2), channel_id=1, source_target_pairs={{0,4},{4,8},{8,12},{12,16},{16,20},{20,24},{24,28},{28,0},{1,5},{5... | collective-permute-start | bytes 1769480 | tf_op jit(solution)/shard_map/ppermute | solution.py:17
  89.6 22.7 %collective-permute-start.7 = (bf16[384]{0:T(512)(128)(2,1)S(1)}, bf16[384]{0:T(512)(128)(2,1)S(1)}, u32[]{:S(2)}, u32[]{:S(2)}) collective-permute-start(bf16[384]{0:T(512)(128)(2,1)S(1)} %collective-permute-done.5), channel_id=1, source_target_pairs={{0,4},{4,8},{8,12},{12,16},{16,20},{20,24},{24,28},{28,0},{1,5},{5... | collective-permute-start | bytes 2312 | tf_op jit(solution)/shard_map/ppermute | solution.py:17
  91.2 21.7 %collective-permute-start.15 = (bf16[384]{0:T(512)(128)(2,1)S(1)}, bf16[384]{0:T(512)(128)(2,1)S(1)}, u32[]{:S(2)}, u32[]{:S(2)}) collective-permute-start(bf16[384]{0:T(512)(128)(2,1)S(1)} %collective-permute-done.13), channel_id=1, source_target_pairs={{0,28},{4,0},{8,4},{12,8},{16,12},{20,16},{24,20},{28,24},{1,29},{... | collective-permute-start | bytes 2312 | tf_op jit(solution)/shard_map/ppermute | solution.py:17
  91.7 24.2 %collective-permute-start.12 = (bf16[384,768]{1,0:T(8,128)(2,1)S(1)}, bf16[384,768]{1,0:T(8,128)(2,1)S(1)}, u32[]{:S(2)}, u32[]{:S(2)}) collective-permute-start(bf16[384,768]{1,0:T(8,128)(2,1)S(1)} %collective-permute-done.10), channel_id=1, source_target_pairs={{0,28},{4,0},{8,4},{12,8},{16,12},{20,16},{24,20},{28,24},{1,29},{... | collective-permute-start | bytes 1769480 | tf_op jit(solution)/shard_map/ppermute | solution.py:17
  114.5 12.0 %collective-permute-start.6 = (bf16[384,768]{1,0:T(8,128)(2,1)S(1)}, bf16[384,768]{1,0:T(8,128)(2,1)S(1)}, u32[]{:S(2)}, u32[]{:S(2)}) collective-permute-start(bf16[384,768]{1,0:T(8,128)(2,1)S(1)} %collective-permute-done.4), channel_id=1, source_target_pairs={{0,4},{4,8},{8,12},{12,16},{16,20},{20,24},{24,28},{28,0},{1,5},{5... | collective-permute-start | bytes 1769480 | tf_op jit(solution)/shard_map/ppermute | solution.py:17
  115.9 30.0 %copy-start.20 = (bf16[384,768]{1,0:T(8,128)(2,1)}, bf16[384,768]{1,0:T(8,128)(2,1)S(1)}, u32[]{:S(2)}) copy-start(bf16[384,768]{1,0:T(8,128)(2,1)S(1)} %collective-permute-done.12) | copy-start | bytes 1769476
  115.9 26.0 %collective-permute-start.14 = (bf16[384,768]{1,0:T(8,128)(2,1)S(1)}, bf16[384,768]{1,0:T(8,128)(2,1)S(1)}, u32[]{:S(2)}, u32[]{:S(2)}) collective-permute-start(bf16[384,768]{1,0:T(8,128)(2,1)S(1)} %collective-permute-done.12), channel_id=1, source_target_pairs={{0,28},{4,0},{8,4},{12,8},{16,12},{20,16},{24,20},{28,24},{1,29},{... | collective-permute-start | bytes 1769480 | tf_op jit(solution)/shard_map/ppermute | solution.py:17
  150.7 34.4 %collective-permute-start.16 = (f32[1,384]{1,0:T(1,128)}, f32[1,384]{1,0:T(1,128)}, u32[]{:S(2)}, u32[]{:S(2)}) collective-permute-start(f32[1,384]{1,0:T(1,128)} %broadcast_in_dim.20), channel_id=1, source_target_pairs={{0,28},{4,0},{8,4},{12,8},{16,12},{20,16},{24,20},{28,24},{1,29},{... | collective-permute-start | bytes 4616 | tf_op jit(solution)/shard_map/ppermute | solution.py:17
  156.7 34.5 %collective-permute-start.20 = (f32[1,384]{1,0:T(1,128)}, f32[1,384]{1,0:T(1,128)}, u32[]{:S(2)}, u32[]{:S(2)}) collective-permute-start(f32[1,384]{1,0:T(1,128)} %broadcast_in_dim.24), channel_id=1, source_target_pairs={{0,4},{4,8},{8,12},{12,16},{16,20},{20,24},{24,28},{28,0},{1,5},{5... | collective-permute-start | bytes 4616 | tf_op jit(solution)/shard_map/ppermute | solution.py:17
  181.2 38.1 %copy-start.27 = (f32[64,384]{1,0:T(8,128)S(1)}, f32[64,384]{1,0:T(8,128)}, u32[]{:S(2)}) copy-start(f32[64,384]{1,0:T(8,128)} %param.7) | copy-start | bytes 294916
  185.1 95.2 %reduce-scatter.5.cloned.1.call-start = ((), (), s32[]{:S(2)}) async-start(), calls=%async_computation.3 | async-start | bytes 491520 | tf_op jit(solution)/shard_map/reduce_scatter | solution.py:58
  185.8 6.7 %collective-permute-start.17 = (f32[1,384]{1,0:T(1,128)S(1)}, f32[1,384]{1,0:T(1,128)S(1)}, u32[]{:S(2)}, u32[]{:S(2)}) collective-permute-start(f32[1,384]{1,0:T(1,128)S(1)} %reshape_add_fusion.5), channel_id=1, source_target_pairs={{0,28},{4,0},{8,4},{12,8},{16,12},{20,16},{24,20},{28,24},{1,29},{... | collective-permute-start | bytes 4616 | tf_op jit(solution)/shard_map/ppermute | solution.py:17
  191.9 4.5 %collective-permute-start.21 = (f32[1,384]{1,0:T(1,128)S(1)}, f32[1,384]{1,0:T(1,128)S(1)}, u32[]{:S(2)}, u32[]{:S(2)}) collective-permute-start(f32[1,384]{1,0:T(1,128)S(1)} %reshape_add_fusion.2), channel_id=1, source_target_pairs={{0,4},{4,8},{8,12},{12,16},{16,20},{20,24},{24,28},{28,0},{1,5},{5... | collective-permute-start | bytes 4616 | tf_op jit(solution)/shard_map/ppermute | solution.py:17
  192.5 4.5 %collective-permute-start.18 = (f32[1,384]{1,0:T(1,128)S(1)}, f32[1,384]{1,0:T(1,128)S(1)}, u32[]{:S(2)}, u32[]{:S(2)}) collective-permute-start(f32[1,384]{1,0:T(1,128)S(1)} %reshape_add_fusion.4), channel_id=1, source_target_pairs={{0,28},{4,0},{8,4},{12,8},{16,12},{20,16},{24,20},{28,24},{1,29},{... | collective-permute-start | bytes 4616 | tf_op jit(solution)/shard_map/ppermute | solution.py:17
  196.4 4.5 %collective-permute-start.22 = (f32[1,384]{1,0:T(1,128)S(1)}, f32[1,384]{1,0:T(1,128)S(1)}, u32[]{:S(2)}, u32[]{:S(2)}) collective-permute-start(f32[1,384]{1,0:T(1,128)S(1)} %reshape_add_fusion.1), channel_id=1, source_target_pairs={{0,4},{4,8},{8,12},{12,16},{16,20},{20,24},{24,28},{28,0},{1,5},{5... | collective-permute-start | bytes 4616 | tf_op jit(solution)/shard_map/ppermute | solution.py:17
  197.0 22.2 %collective-permute-start.19 = (f32[1,384]{1,0:T(1,128)S(1)}, f32[1,384]{1,0:T(1,128)S(1)}, u32[]{:S(2)}, u32[]{:S(2)}) collective-permute-start(f32[1,384]{1,0:T(1,128)S(1)} %reshape_add_fusion.3), channel_id=1, source_target_pairs={{0,28},{4,0},{8,4},{12,8},{16,12},{20,16},{24,20},{28,24},{1,29},{... | collective-permute-start | bytes 4616 | tf_op jit(solution)/shard_map/ppermute | solution.py:17
  200.9 18.4 %collective-permute-start.23 = (f32[1,384]{1,0:T(1,128)S(1)}, f32[1,384]{1,0:T(1,128)S(1)}, u32[]{:S(2)}, u32[]{:S(2)}) collective-permute-start(f32[1,384]{1,0:T(1,128)S(1)} %reshape_add_fusion), channel_id=1, source_target_pairs={{0,4},{4,8},{8,12},{12,16},{16,20},{20,24},{24,28},{28,0},{1,5},{5... | collective-permute-start | bytes 4616 | tf_op jit(solution)/shard_map/ppermute | solution.py:17
  225.0 9.4 %collective-permute-start.24 = (bf16[64,384]{1,0:T(8,128)(2,1)S(1)}, bf16[64,384]{1,0:T(8,128)(2,1)S(1)}, u32[]{:S(2)}, u32[]{:S(2)}) collective-permute-start(bf16[64,384]{1,0:T(8,128)(2,1)S(1)} %multiply_convert_fusion), channel_id=1, source_target_pairs={{0,4},{4,8},{8,12},{12,16},{16,20},{20,24},{24,28},{28,0},{1,5},{5... | collective-permute-start | bytes 147464 | tf_op jit(solution)/shard_map/ppermute | solution.py:17
  226.5 10.0 %collective-permute-start.28 = (bf16[64,384]{1,0:T(8,128)(2,1)S(1)}, bf16[64,384]{1,0:T(8,128)(2,1)S(1)}, u32[]{:S(2)}, u32[]{:S(2)}) collective-permute-start(bf16[64,384]{1,0:T(8,128)(2,1)S(1)} %multiply_convert_fusion), channel_id=1, source_target_pairs={{0,28},{4,0},{8,4},{12,8},{16,12},{20,16},{24,20},{28,24},{1,29},{... | collective-permute-start | bytes 147464 | tf_op jit(solution)/shard_map/ppermute | solution.py:17
  230.6 11.7 %collective-permute-start.32 = (f32[64,384]{1,0:T(8,128)S(1)}, f32[64,384]{1,0:T(8,128)S(1)}, u32[]{:S(2)}, u32[]{:S(2)}) collective-permute-start(f32[64,384]{1,0:T(8,128)S(1)} %fusion.18), channel_id=1, source_target_pairs={{0,28},{4,0},{8,4},{12,8},{16,12},{20,16},{24,20},{28,24},{1,29},{... | collective-permute-start | bytes 294920 | tf_op jit(solution)/shard_map/ppermute | solution.py:17
  232.4 20.6 %collective-permute-start.36 = (f32[64,384]{1,0:T(8,128)S(1)}, f32[64,384]{1,0:T(8,128)S(1)}, u32[]{:S(2)}, u32[]{:S(2)}) collective-permute-start(f32[64,384]{1,0:T(8,128)S(1)} %fusion.6), channel_id=1, source_target_pairs={{0,4},{4,8},{8,12},{12,16},{16,20},{20,24},{24,28},{28,0},{1,5},{5... | collective-permute-start | bytes 294920 | tf_op jit(solution)/shard_map/ppermute | solution.py:17
  234.5 5.3 %collective-permute-start.25 = (bf16[64,384]{1,0:T(8,128)(2,1)S(1)}, bf16[64,384]{1,0:T(8,128)(2,1)S(1)}, u32[]{:S(2)}, u32[]{:S(2)}) collective-permute-start(bf16[64,384]{1,0:T(8,128)(2,1)S(1)} %collective-permute-done.24), channel_id=1, source_target_pairs={{0,4},{4,8},{8,12},{12,16},{16,20},{20,24},{24,28},{28,0},{1,5},{5... | collective-permute-start | bytes 147464 | tf_op jit(solution)/shard_map/ppermute | solution.py:17
  236.5 5.1 %collective-permute-start.29 = (bf16[64,384]{1,0:T(8,128)(2,1)S(1)}, bf16[64,384]{1,0:T(8,128)(2,1)S(1)}, u32[]{:S(2)}, u32[]{:S(2)}) collective-permute-start(bf16[64,384]{1,0:T(8,128)(2,1)S(1)} %collective-permute-done.28), channel_id=1, source_target_pairs={{0,28},{4,0},{8,4},{12,8},{16,12},{20,16},{24,20},{28,24},{1,29},{... | collective-permute-start | bytes 147464 | tf_op jit(solution)/shard_map/ppermute | solution.py:17
  239.7 4.6 %collective-permute-start.26 = (bf16[64,384]{1,0:T(8,128)(2,1)S(1)}, bf16[64,384]{1,0:T(8,128)(2,1)S(1)}, u32[]{:S(2)}, u32[]{:S(2)}) collective-permute-start(bf16[64,384]{1,0:T(8,128)(2,1)S(1)} %collective-permute-done.25), channel_id=1, source_target_pairs={{0,4},{4,8},{8,12},{12,16},{16,20},{20,24},{24,28},{28,0},{1,5},{5... | collective-permute-start | bytes 147464 | tf_op jit(solution)/shard_map/ppermute | solution.py:17
  241.6 5.2 %collective-permute-start.30 = (bf16[64,384]{1,0:T(8,128)(2,1)S(1)}, bf16[64,384]{1,0:T(8,128)(2,1)S(1)}, u32[]{:S(2)}, u32[]{:S(2)}) collective-permute-start(bf16[64,384]{1,0:T(8,128)(2,1)S(1)} %collective-permute-done.29), channel_id=1, source_target_pairs={{0,28},{4,0},{8,4},{12,8},{16,12},{20,16},{24,20},{28,24},{1,29},{... | collective-permute-start | bytes 147464 | tf_op jit(solution)/shard_map/ppermute | solution.py:17
  242.6 14.6 %collective-permute-start.33 = (f32[64,384]{1,0:T(8,128)S(1)}, f32[64,384]{1,0:T(8,128)S(1)}, u32[]{:S(2)}, u32[]{:S(2)}) collective-permute-start(f32[64,384]{1,0:T(8,128)S(1)} %convolution_add_fusion.8), channel_id=1, source_target_pairs={{0,28},{4,0},{8,4},{12,8},{16,12},{20,16},{24,20},{28,24},{1,29},{... | collective-permute-start | bytes 294920 | tf_op jit(solution)/shard_map/ppermute | solution.py:17
  244.3 5.0 %collective-permute-start.27 = (bf16[64,384]{1,0:T(8,128)(2,1)S(1)}, bf16[64,384]{1,0:T(8,128)(2,1)S(1)}, u32[]{:S(2)}, u32[]{:S(2)}) collective-permute-start(bf16[64,384]{1,0:T(8,128)(2,1)S(1)} %collective-permute-done.26), channel_id=1, source_target_pairs={{0,4},{4,8},{8,12},{12,16},{16,20},{20,24},{24,28},{28,0},{1,5},{5... | collective-permute-start | bytes 147464 | tf_op jit(solution)/shard_map/ppermute | solution.py:17
  246.8 5.0 %collective-permute-start.31 = (bf16[64,384]{1,0:T(8,128)(2,1)S(1)}, bf16[64,384]{1,0:T(8,128)(2,1)S(1)}, u32[]{:S(2)}, u32[]{:S(2)}) collective-permute-start(bf16[64,384]{1,0:T(8,128)(2,1)S(1)} %collective-permute-done.30), channel_id=1, source_target_pairs={{0,28},{4,0},{8,4},{12,8},{16,12},{20,16},{24,20},{28,24},{1,29},{... | collective-permute-start | bytes 147464 | tf_op jit(solution)/shard_map/ppermute | solution.py:17
  254.7 6.5 %collective-permute-start.37 = (f32[64,384]{1,0:T(8,128)S(1)}, f32[64,384]{1,0:T(8,128)S(1)}, u32[]{:S(2)}, u32[]{:S(2)}) collective-permute-start(f32[64,384]{1,0:T(8,128)S(1)} %convolution_add_fusion.7), channel_id=1, source_target_pairs={{0,4},{4,8},{8,12},{12,16},{16,20},{20,24},{24,28},{28,0},{1,5},{5... | collective-permute-start | bytes 294920 | tf_op jit(solution)/shard_map/ppermute | solution.py:17
  257.2 7.1 %collective-permute-start.34 = (f32[64,384]{1,0:T(8,128)S(1)}, f32[64,384]{1,0:T(8,128)S(1)}, u32[]{:S(2)}, u32[]{:S(2)}) collective-permute-start(f32[64,384]{1,0:T(8,128)S(1)} %add.427), channel_id=1, source_target_pairs={{0,28},{4,0},{8,4},{12,8},{16,12},{20,16},{24,20},{28,24},{1,29},{... | collective-permute-start | bytes 294920 | tf_op jit(solution)/shard_map/ppermute | solution.py:17
  261.2 6.4 %collective-permute-start.38 = (f32[64,384]{1,0:T(8,128)S(1)}, f32[64,384]{1,0:T(8,128)S(1)}, u32[]{:S(2)}, u32[]{:S(2)}) collective-permute-start(f32[64,384]{1,0:T(8,128)S(1)} %add.431), channel_id=1, source_target_pairs={{0,4},{4,8},{8,12},{12,16},{16,20},{20,24},{24,28},{28,0},{1,5},{5... | collective-permute-start | bytes 294920 | tf_op jit(solution)/shard_map/ppermute | solution.py:17
  264.3 7.6 %collective-permute-start.35 = (f32[64,384]{1,0:T(8,128)S(1)}, f32[64,384]{1,0:T(8,128)S(1)}, u32[]{:S(2)}, u32[]{:S(2)}) collective-permute-start(f32[64,384]{1,0:T(8,128)S(1)} %add.428), channel_id=1, source_target_pairs={{0,28},{4,0},{8,4},{12,8},{16,12},{20,16},{24,20},{28,24},{1,29},{... | collective-permute-start | bytes 294920 | tf_op jit(solution)/shard_map/ppermute | solution.py:17
  267.7 5.3 %collective-permute-start.39 = (f32[64,384]{1,0:T(8,128)S(1)}, f32[64,384]{1,0:T(8,128)S(1)}, u32[]{:S(2)}, u32[]{:S(2)}) collective-permute-start(f32[64,384]{1,0:T(8,128)S(1)} %add.432), channel_id=1, source_target_pairs={{0,4},{4,8},{8,12},{12,16},{16,20},{20,24},{24,28},{28,0},{1,5},{5... | collective-permute-start | bytes 294920 | tf_op jit(solution)/shard_map/ppermute | solution.py:17
  (44 other events, 280.3 us)
Sparse Core Ops, SparseCore 0:
  8.9 25.1 all-gather.1
  185.2 32.9 reduce-scatter.6
  253.1 27.1 reduce-scatter.4
where the time goes:
time: 345 us; the launch traced here: 344 us
  waiting for transfers between devices  99 us (29%)
  other arithmetic  73.4 us (21%)
  starting transfers between devices  55.6 us (16%)
  blocking collectives  49 us (14%)
  matrix products  47.9 us (14%)
  between operations  13.8 us (4%)
  local copies, waits for them, and re-layouts  5.73 us (2%)
    ppermute x40, waiting for transfers between devices, shifted(): return lax.ppermute(value, axis, pairs)  73.5 us
    ppermute x40, starting transfers between devices, shifted(): return lax.ppermute(value, axis, pairs)  55.5 us
    reduce_sum x1, other arithmetic, pair_weights(): jnp.sum((lists_here[:, :, None] == positions[None, None, :]).astype(jnp.f...  44.8 us
    psum x1, blocking collectives, local(): gram = lax.psum(partial_gram, ('blk', 'sub'))  43.3 us
    dot_general x9, matrix products, pair_weights(): lax.dot_general(block_feats, moving_feats, (((1,), (1,)), ((), ())), pref...  33.6 us
    unnamed x4, waiting for transfers between devices  18.1 us
    dot_general x9, matrix products, product_work(): col_term = jnp.dot(block_eigen, tile, preferred_element_type=jnp.float32)  8.02 us
    reduce_scatter x1, waiting for transfers between devices, to_owners(): return lax.psum_scatter(terms, 'sub', scatter_dimension=1, tiled=True)  7.33 us
  transfers between devices with their start and end apart: 43, of which 20 were waited for; matrix products, arithmetic and copies ran while one was open for 30% of the time, Pallas kernels for 0%

commit v1 on v0

--- a/solution.py
+++ b/solution.py
@@ -105,7 +105,7 @@
     partial_gram = jnp.dot(
         mixed, mixed.T, precision=lax.Precision.HIGHEST, preferred_element_type=jnp.float32
     )
-    gram = lax.psum(partial_gram, ("blk", "sub"))
+    gram = lax.psum(lax.psum(partial_gram, "sub"), "blk")
     lower = jnp.linalg.cholesky(gram)
     total_rows = rows_dev * lax.axis_size("blk") * lax.axis_size("sub")
     return math.sqrt(total_rows) * jax.scipy.linalg.solve_triangular(lower, mixed, lower=True)

time: 345 us -> 351 us (1.017); the launches traced: 344 us -> 345 us
    psum x1 -> x2, blocking collectives: 43.3 us -> 43.4 us  [local(): gram = lax.psum(lax.psum(partial_gram, 'sub'), 'blk')]
where the time goes in v1:
time: 351 us; the launch traced here: 345 us
  waiting for transfers between devices  99 us (28%)
  other arithmetic  73.4 us (21%)
  starting transfers between devices  55.6 us (16%)
  blocking collectives  49.2 us (14%)
  matrix products  47.9 us (14%)
  between operations  13.8 us (4%)
  local copies, waits for them, and re-layouts  5.73 us (2%)
    ppermute x40, waiting for transfers between devices, shifted(): return lax.ppermute(value, axis, pairs)  73.5 us
    ppermute x40, starting transfers between devices, shifted(): return lax.ppermute(value, axis, pairs)  55.5 us
    reduce_sum x1, other arithmetic, pair_weights(): jnp.sum((lists_here[:, :, None] == positions[None, None, :]).astype(jnp.f...  44.8 us
    psum x2, blocking collectives, local(): gram = lax.psum(lax.psum(partial_gram, 'sub'), 'blk')  43.4 us
    dot_general x9, matrix products, pair_weights(): lax.dot_general(block_feats, moving_feats, (((1,), (1,)), ((), ())), pref...  33.6 us
    unnamed x4, waiting for transfers between devices  18.1 us
    dot_general x9, matrix products, product_work(): col_term = jnp.dot(block_eigen, tile, preferred_element_type=jnp.float32)  8.02 us
    reduce_scatter x1, waiting for transfers between devices, to_owners(): return lax.psum_scatter(terms, 'sub', scatter_dimension=1, tiled=True)  7.33 us
  transfers between devices with their start and end apart: 43, of which 20 were waited for; matrix products, arithmetic and copies ran while one was open for 30% of the time, Pallas kernels for 0%

profile of v1, /device:TPU:10, one launch (start us, length us, event | category | flops | bytes accessed | tf_op | source)
XLA Modules:
  0.0 344.6 jit_solution(16006190981055517272)
XLA Ops:
  7.3 1.6 collective-permute-start
  15.0 20.4 %collective-permute-done.1 = bf16[384]{0:T(512)(128)(2,1)S(1)} collective-permute-done((bf16[384]{0:T(512)(128)(2,1)S(1)}, bf16[384]{0:T(512)(128)(2,1)S(1)}, u32[]{:S(2)}, u32[]{:S(2)}) %collective-permute-start.1) | collective-permute-done | bytes 800 | tf_op jit(solution)/shard_map/ppermute | solution.py:17
  37.4 1.5 collective-permute-start.2
  39.4 44.8 %convert_reduce_fusion.7 = (f32[1536,384]{1,0:T(8,128)}, f32[1536,384]{1,0:T(8,128)}, f32[1536,384]{1,0:T(8,128)}, f32[1536,384]{1,0:T(8,128)}, f32[1536,384]{1,...) fusion(s32[16,1536]{1,0:T(8,128)S(1)} %get-tuple-element.40, ...), kind=kLoop, calls=%fused_computation.7 | loop fusion | flops 249495552 | bytes 22119936 | tf_op jit(solution)/shard_map/reduce_sum | solution.py:30
  84.3 2.4 collective-permute-start.5
  86.7 2.9 collective-permute-start.4
  89.6 1.5 collective-permute-start.7
  91.7 1.8 collective-permute-start.12
  97.1 15.2 %collective-permute-done.7 = bf16[384]{0:T(512)(128)(2,1)S(1)} collective-permute-done((bf16[384]{0:T(512)(128)(2,1)S(1)}, bf16[384]{0:T(512)(128)(2,1)S(1)}, u32[]{:S(2)}, u32[]{:S(2)}) %collective-permute-start.7) | collective-permute-done | bytes 800 | tf_op jit(solution)/shard_map/ppermute | solution.py:17
  119.7 6.8 %collective-permute-done.6 = bf16[384,768]{1,0:T(8,128)(2,1)S(1)} collective-permute-done((bf16[384,768]{1,0:T(8,128)(2,1)S(1)}, bf16[384,768]{1,0:T(8,128)(2,1)S(1)}, u32[]{:S(2)}, u32[]{:S(2)}) %collective-permute-start.6) | collective-permute-done | bytes 589856 | tf_op jit(solution)/shard_map/ppermute | solution.py:17
  127.3 14.6 %collective-permute-done.14 = bf16[384,768]{1,0:T(8,128)(2,1)S(1)} collective-permute-done((bf16[384,768]{1,0:T(8,128)(2,1)S(1)}, bf16[384,768]{1,0:T(8,128)(2,1)S(1)}, u32[]{:S(2)}, u32[]{:S(2)}) %collective-permute-start.14) | collective-permute-done | bytes 589856 | tf_op jit(solution)/shard_map/ppermute | solution.py:17
  143.5 2.3 multiply_reduce_fusion
  145.9 4.2 %fusion.40 = (f32[384]{0:T(512)S(1)}, f32[1536]{0:T(1024)S(1)}, bf16[1536,384]{1,0:T(8,128)(2,1)S(1)}) fusion(f32[1536,384]{1,0:T(8,128)} %get-tuple-element.26, f32[384]{0:T(512)} %convert_element_type.159, f32[1536]{0:T(1024)S(1)} %convert_multiply_fusion, bf16[1536,768]{1,0:T(8,128)(2,1)S(1)} %copy-done.8, bf16[384,768]{1,0:T(8,128)(2,1)} %copy-done.26, ...), kind=kOutput, calls=%fused_computation.114 | convolution fusion | flops 911865984 | bytes 6511104 | tf_op jit(solution)/shard_map/dot_general | solution.py:23
  150.7 2.0 collective-permute-start.16
  152.7 3.4 fusion.44
  157.7 4.0 %fusion.39 = (f32[384]{0:T(512)}, f32[1536]{0:T(1024)S(1)}, bf16[1536,384]{1,0:T(8,128)(2,1)}) fusion(f32[1536,384]{1,0:T(8,128)S(1)} %copy-done.16, f32[384]{0:T(512)S(1)} %copy-done.41, f32[1536]{0:T(1024)S(1)} %convert_multiply_fusion, bf16[1536,768]{1,0:T(8,128)(2,1)S(1)} %copy-done.8, bf16[384,768]{1,0:T(8,128)(2,1)S(1)} %copy-done.23, ...), kind=kOutput, calls=%fused_computation.113 | convolution fusion | flops 911865984 | bytes 6511104 | tf_op jit(solution)/shard_map/dot_general | solution.py:23
  161.7 4.0 %fusion.38 = (f32[384]{0:T(512)}, f32[1536]{0:T(1024)S(1)}, bf16[1536,384]{1,0:T(8,128)(2,1)}) fusion(f32[1536,384]{1,0:T(8,128)S(1)} %copy-done.15, f32[384]{0:T(512)S(1)} %copy-done.40, f32[1536]{0:T(1024)S(1)} %convert_multiply_fusion, bf16[1536,768]{1,0:T(8,128)(2,1)S(1)} %copy-done.8, bf16[384,768]{1,0:T(8,128)(2,1)S(1)} %copy-done.19, ...), kind=kOutput, calls=%fused_computation.112 | convolution fusion | flops 911865984 | bytes 6511104 | tf_op jit(solution)/shard_map/dot_general | solution.py:23
  165.7 3.9 %fusion.37 = (f32[384]{0:T(512)}, f32[1536]{0:T(1024)S(1)}, bf16[1536,384]{1,0:T(8,128)(2,1)}) fusion(f32[1536,384]{1,0:T(8,128)S(1)} %copy-done.14, f32[384]{0:T(512)S(1)} %copy-done.38, f32[1536]{0:T(1024)S(1)} %convert_multiply_fusion, bf16[1536,768]{1,0:T(8,128)(2,1)S(1)} %copy-done.8, bf16[384,768]{1,0:T(8,128)(2,1)S(1)} %collective-permute-done, ...), kind=kOutput, calls=%fused_computation.111 | convolution fusion | flops 911865984 | bytes 6511104 | tf_op jit(solution)/shard_map/dot_general | solution.py:23
  169.7 3.9 %fusion.43 = (f32[384]{0:T(512)}, f32[1536]{0:T(1024)S(1)}, bf16[1536,384]{1,0:T(8,128)(2,1)}) fusion(f32[1536,384]{1,0:T(8,128)S(1)} %copy-done.13, f32[384]{0:T(512)S(1)} %copy-done.39, f32[1536]{0:T(1024)S(1)} %convert_multiply_fusion, bf16[1536,768]{1,0:T(8,128)(2,1)S(1)} %copy-done.8, bf16[384,768]{1,0:T(8,128)(2,1)S(1)} %copy-done.21, ...), kind=kOutput, calls=%fused_computation.117 | convolution fusion | flops 911865984 | bytes 6511104 | tf_op jit(solution)/shard_map/dot_general | solution.py:23
  173.7 4.1 %fusion.42 = (f32[384]{0:T(512)}, f32[1536]{0:T(1024)S(1)}, bf16[1536,384]{1,0:T(8,128)(2,1)}) fusion(f32[1536,384]{1,0:T(8,128)S(1)} %copy-done.12, f32[384]{0:T(512)S(1)} %copy-done.37, f32[1536]{0:T(1024)S(1)} %convert_multiply_fusion, bf16[1536,768]{1,0:T(8,128)(2,1)S(1)} %copy-done.8, bf16[384,768]{1,0:T(8,128)(2,1)S(1)} %collective-permute-done.10, ...), kind=kOutput, calls=%fused_computation.116 | convolution fusion | flops 911865984 | bytes 6511104 | tf_op jit(solution)/shard_map/dot_general | solution.py:23
  177.7 3.4 fusion.41
  181.2 2.6 fusion.36
  185.8 5.4 %collective-permute-start.17 = (f32[1,384]{1,0:T(1,128)S(1)}, f32[1,384]{1,0:T(1,128)S(1)}, u32[]{:S(2)}, u32[]{:S(2)}) collective-permute-start(f32[1,384]{1,0:T(1,128)S(1)} %reshape_add_fusion.5), channel_id=1, source_target_pairs={{0,28},{4,0},{8,4},{12,8},{16,12},{20,16},{24,20},{28,24},{1,29},{... | collective-permute-start | bytes 4616 | tf_op jit(solution)/shard_map/ppermute | solution.py:17
  192.5 2.9 collective-permute-start.18
  197.0 2.9 collective-permute-start.19
  200.9 17.3 %reduce-scatter.7.cloned.1.call-done = f32[384,1]{1,0:T(8,128)} async-done(((f32[1536,1]{1,0:T(8,128)}), f32[384,1]{1,0:T(8,128)}) %reduce-scatter.7.cloned.1.call-update) | async-done | bytes 1552
  219.3 5.7 %all_gather.7 = bf16[64,1536]{1,0:T(8,128)(2,1)S(1)} all-gather(bf16[64,384]{1,0:T(8,128)(2,1)S(1)} %multiply_convert_fusion), channel_id=1, replica_groups=mesh['blk'=8,'sub'=4] {'sub'}, dimensions={1}, use_global_device_ids=true | all-gather | bytes 245760 | tf_op jit(solution)/shard_map/all_gather | solution.py:91
  227.1 1.6 fusion.26
  228.7 1.6 fusion.23
  230.6 1.5 collective-permute-start.32
  232.4 1.5 collective-permute-start.36
  234.5 1.5 collective-permute-start.25
  237.6 2.1 collective-permute-done.25
  242.6 1.6 collective-permute-start.33
  244.3 1.8 collective-permute-start.27
  247.4 1.9 collective-permute-done.27
  253.0 1.7 convolution_add_fusion.7
  255.6 1.6 fusion.11
  257.2 2.6 collective-permute-start.34
  261.6 2.7 collective-permute-done.34
  264.3 2.5 collective-permute-start.35
  267.7 1.7 collective-permute-start.39
  269.7 2.2 collective-permute-done.35
  273.0 7.3 %reduce-scatter.5.cloned.1.call-done = f32[64,384]{1,0:T(8,128)} async-done(((f32[64,1536]{1,0:T(8,128)}), f32[64,384]{1,0:T(8,128)}) %reduce-scatter.5.cloned.1.call-update) | async-done | bytes 98320 | tf_op jit(solution)/shard_map/reduce_scatter | solution.py:58
  281.5 10.4 %psum.14 = f32[64,64]{0,1:T(8,128)S(1)} all-reduce(f32[64,64]{0,1:T(8,128)S(1)} %fusion.46), channel_id=1, replica_groups=mesh['blk'=8,'sub'=4] {'sub'}, use_global_device_ids=true, to_apply=%region_39.0 | all-reduce | flops 4096 | bytes 32768 | tf_op jit(solution)/shard_map/psum | solution.py:108
  291.9 33.0 %psum.15 = f32[64,64]{0,1:T(8,128)S(1)} all-reduce(f32[64,64]{0,1:T(8,128)S(1)} %psum.14), channel_id=1, replica_groups=mesh['blk'=8,'sub'=4] {'blk'}, use_global_device_ids=true, to_apply=%region_40.0 | all-reduce | flops 4096 | bytes 32768 | tf_op jit(solution)/shard_map/psum | solution.py:108
  325.0 5.8 %cholesky.16 = f32[64,64]{1,0:T(8,128)S(1)} custom-call(f32[64,64]{1,0:T(8,128)S(1)} %fusion.35), custom_call_target="Cholesky" | custom-call | tf_op jit(solution)/shard_map/jit(cholesky)/cholesky | solution.py:109
  332.2 4.9 %custom-call.7 = f32[1,64,64]{1,2,0:T(8,128)S(1)} custom-call(f32[1,64,64]{2,1,0:T(8,128)S(1)} %fusion.33), custom_call_target="InvertDiagBlocksLowerTriangular" | custom-call | tf_op jit(solution)/shard_map/jit(_solve_triangular)/triangular_solve | solution.py:111
  (219 shorter events, 53.3 us)
Async XLA Ops:
  6.5 136.9 %all-gather.2.cloned.1.call-start = ((), (), s32[]{:S(2)}) async-start(), calls=%async_computation.2 | async-start | bytes 2949120 | tf_op jit(solution)/shard_map/all_gather | solution.py:65
  7.3 210.9 %reduce-scatter.7.cloned.1.call-start = ((), (), s32[]{:S(2)}) async-start(), calls=%async_computation.4 | async-start | bytes 983040
  7.3 30.1 %collective-permute-start = (bf16[384,768]{1,0:T(8,128)(2,1)}, bf16[384,768]{1,0:T(8,128)(2,1)S(1)}, u32[]{:S(2)}, u32[]{:S(2)}) collective-permute-start(bf16[384,768]{1,0:T(8,128)(2,1)} %param.4), channel_id=1, source_target_pairs={{0,4},{4,8},{8,12},{12,16},{16,20},{20,24},{24,28},{28,0},{1,5},{5... | collective-permute-start | bytes 1769480 | tf_op jit(solution)/shard_map/ppermute | solution.py:17
  10.2 25.1 %collective-permute-start.1 = (bf16[384]{0:T(512)(128)(2,1)S(1)}, bf16[384]{0:T(512)(128)(2,1)S(1)}, u32[]{:S(2)}, u32[]{:S(2)}) collective-permute-start(bf16[384]{0:T(512)(128)(2,1)S(1)} %get-tuple-element.33), channel_id=1, source_target_pairs={{0,4},{4,8},{8,12},{12,16},{16,20},{20,24},{24,28},{28,0},{1,5},{5... | collective-permute-start | bytes 2312 | tf_op jit(solution)/shard_map/ppermute | solution.py:17
  11.7 24.2 %collective-permute-start.9 = (bf16[384]{0:T(512)(128)(2,1)S(1)}, bf16[384]{0:T(512)(128)(2,1)S(1)}, u32[]{:S(2)}, u32[]{:S(2)}) collective-permute-start(bf16[384]{0:T(512)(128)(2,1)S(1)} %get-tuple-element.33), channel_id=1, source_target_pairs={{0,28},{4,0},{8,4},{12,8},{16,12},{20,16},{24,20},{28,24},{1,29},{... | collective-permute-start | bytes 2312 | tf_op jit(solution)/shard_map/ppermute | solution.py:17
  12.3 26.6 %collective-permute-start.8 = (bf16[384,768]{1,0:T(8,128)(2,1)}, bf16[384,768]{1,0:T(8,128)(2,1)S(1)}, u32[]{:S(2)}, u32[]{:S(2)}) collective-permute-start(bf16[384,768]{1,0:T(8,128)(2,1)} %param.4), channel_id=1, source_target_pairs={{0,28},{4,0},{8,4},{12,8},{16,12},{20,16},{24,20},{28,24},{1,29},{... | collective-permute-start | bytes 1769480 | tf_op jit(solution)/shard_map/ppermute | solution.py:17
  35.4 48.9 %collective-permute-start.3 = (bf16[384]{0:T(512)(128)(2,1)S(1)}, bf16[384]{0:T(512)(128)(2,1)S(1)}, u32[]{:S(2)}, u32[]{:S(2)}) collective-permute-start(bf16[384]{0:T(512)(128)(2,1)S(1)} %collective-permute-done.1), channel_id=1, source_target_pairs={{0,4},{4,8},{8,12},{12,16},{16,20},{20,24},{24,28},{28,0},{1,5},{5... | collective-permute-start | bytes 2312 | tf_op jit(solution)/shard_map/ppermute | solution.py:17
  36.0 50.7 %collective-permute-start.11 = (bf16[384]{0:T(512)(128)(2,1)S(1)}, bf16[384]{0:T(512)(128)(2,1)S(1)}, u32[]{:S(2)}, u32[]{:S(2)}) collective-permute-start(bf16[384]{0:T(512)(128)(2,1)S(1)} %collective-permute-done.9), channel_id=1, source_target_pairs={{0,28},{4,0},{8,4},{12,8},{16,12},{20,16},{24,20},{28,24},{1,29},{... | collective-permute-start | bytes 2312 | tf_op jit(solution)/shard_map/ppermute | solution.py:17
  37.4 49.3 %collective-permute-start.2 = (bf16[384,768]{1,0:T(8,128)(2,1)S(1)}, bf16[384,768]{1,0:T(8,128)(2,1)S(1)}, u32[]{:S(2)}, u32[]{:S(2)}) collective-permute-start(bf16[384,768]{1,0:T(8,128)(2,1)S(1)} %collective-permute-done), channel_id=1, source_target_pairs={{0,4},{4,8},{8,12},{12,16},{16,20},{20,24},{24,28},{28,0},{1,5},{5... | collective-permute-start | bytes 1769480 | tf_op jit(solution)/shard_map/ppermute | solution.py:17
  38.9 52.8 %collective-permute-start.10 = (bf16[384,768]{1,0:T(8,128)(2,1)S(1)}, bf16[384,768]{1,0:T(8,128)(2,1)S(1)}, u32[]{:S(2)}, u32[]{:S(2)}) collective-permute-start(bf16[384,768]{1,0:T(8,128)(2,1)S(1)} %collective-permute-done.8), channel_id=1, source_target_pairs={{0,28},{4,0},{8,4},{12,8},{16,12},{20,16},{24,20},{28,24},{1,29},{... | collective-permute-start | bytes 1769480 | tf_op jit(solution)/shard_map/ppermute | solution.py:17
  39.4 50.2 %copy-start.28 = (bf16[1536]{0:T(1024)(128)(2,1)S(1)}, bf16[1536]{0:T(1024)(128)(2,1)}, u32[]{:S(2)}) copy-start(bf16[1536]{0:T(1024)(128)(2,1)} %param.5) | copy-start | bytes 9220
  39.4 54.0 %copy-start.9 = (bf16[384,768]{1,0:T(8,128)(2,1)S(1)}, bf16[384,768]{1,0:T(8,128)(2,1)}, u32[]{:S(2)}) copy-start(bf16[384,768]{1,0:T(8,128)(2,1)} %param.4) | copy-start | bytes 1769476
  84.3 5.4 %collective-permute-start.5 = (bf16[384]{0:T(512)(128)(2,1)S(1)}, bf16[384]{0:T(512)(128)(2,1)S(1)}, u32[]{:S(2)}, u32[]{:S(2)}) collective-permute-start(bf16[384]{0:T(512)(128)(2,1)S(1)} %collective-permute-done.3), channel_id=1, source_target_pairs={{0,4},{4,8},{8,12},{12,16},{16,20},{20,24},{24,28},{28,0},{1,5},{5... | collective-permute-start | bytes 2312 | tf_op jit(solution)/shard_map/ppermute | solution.py:17
  86.7 4.5 %collective-permute-start.13 = (bf16[384]{0:T(512)(128)(2,1)S(1)}, bf16[384]{0:T(512)(128)(2,1)S(1)}, u32[]{:S(2)}, u32[]{:S(2)}) collective-permute-start(bf16[384]{0:T(512)(128)(2,1)S(1)} %collective-permute-done.11), channel_id=1, source_target_pairs={{0,28},{4,0},{8,4},{12,8},{16,12},{20,16},{24,20},{28,24},{1,29},{... | collective-permute-start | bytes 2312 | tf_op jit(solution)/shard_map/ppermute | solution.py:17
  86.7 40.6 %copy-start.18 = (bf16[384,768]{1,0:T(8,128)(2,1)}, bf16[384,768]{1,0:T(8,128)(2,1)S(1)}, u32[]{:S(2)}) copy-start(bf16[384,768]{1,0:T(8,128)(2,1)S(1)} %collective-permute-done.2) | copy-start | bytes 1769476
  86.7 27.8 %collective-permute-start.4 = (bf16[384,768]{1,0:T(8,128)(2,1)S(1)}, bf16[384,768]{1,0:T(8,128)(2,1)S(1)}, u32[]{:S(2)}, u32[]{:S(2)}) collective-permute-start(bf16[384,768]{1,0:T(8,128)(2,1)S(1)} %collective-permute-done.2), channel_id=1, source_target_pairs={{0,4},{4,8},{8,12},{12,16},{16,20},{20,24},{24,28},{28,0},{1,5},{5... | collective-permute-start | bytes 1769480 | tf_op jit(solution)/shard_map/ppermute | solution.py:17
  89.6 22.7 %collective-permute-start.7 = (bf16[384]{0:T(512)(128)(2,1)S(1)}, bf16[384]{0:T(512)(128)(2,1)S(1)}, u32[]{:S(2)}, u32[]{:S(2)}) collective-permute-start(bf16[384]{0:T(512)(128)(2,1)S(1)} %collective-permute-done.5), channel_id=1, source_target_pairs={{0,4},{4,8},{8,12},{12,16},{16,20},{20,24},{24,28},{28,0},{1,5},{5... | collective-permute-start | bytes 2312 | tf_op jit(solution)/shard_map/ppermute | solution.py:17
  91.2 21.7 %collective-permute-start.15 = (bf16[384]{0:T(512)(128)(2,1)S(1)}, bf16[384]{0:T(512)(128)(2,1)S(1)}, u32[]{:S(2)}, u32[]{:S(2)}) collective-permute-start(bf16[384]{0:T(512)(128)(2,1)S(1)} %collective-permute-done.13), channel_id=1, source_target_pairs={{0,28},{4,0},{8,4},{12,8},{16,12},{20,16},{24,20},{28,24},{1,29},{... | collective-permute-start | bytes 2312 | tf_op jit(solution)/shard_map/ppermute | solution.py:17
  91.7 24.2 %collective-permute-start.12 = (bf16[384,768]{1,0:T(8,128)(2,1)S(1)}, bf16[384,768]{1,0:T(8,128)(2,1)S(1)}, u32[]{:S(2)}, u32[]{:S(2)}) collective-permute-start(bf16[384,768]{1,0:T(8,128)(2,1)S(1)} %collective-permute-done.10), channel_id=1, source_target_pairs={{0,28},{4,0},{8,4},{12,8},{16,12},{20,16},{24,20},{28,24},{1,29},{... | collective-permute-start | bytes 1769480 | tf_op jit(solution)/shard_map/ppermute | solution.py:17
  114.5 12.0 %collective-permute-start.6 = (bf16[384,768]{1,0:T(8,128)(2,1)S(1)}, bf16[384,768]{1,0:T(8,128)(2,1)S(1)}, u32[]{:S(2)}, u32[]{:S(2)}) collective-permute-start(bf16[384,768]{1,0:T(8,128)(2,1)S(1)} %collective-permute-done.4), channel_id=1, source_target_pairs={{0,4},{4,8},{8,12},{12,16},{16,20},{20,24},{24,28},{28,0},{1,5},{5... | collective-permute-start | bytes 1769480 | tf_op jit(solution)/shard_map/ppermute | solution.py:17
  115.9 30.0 %copy-start.20 = (bf16[384,768]{1,0:T(8,128)(2,1)}, bf16[384,768]{1,0:T(8,128)(2,1)S(1)}, u32[]{:S(2)}) copy-start(bf16[384,768]{1,0:T(8,128)(2,1)S(1)} %collective-permute-done.12) | copy-start | bytes 1769476
  115.9 26.0 %collective-permute-start.14 = (bf16[384,768]{1,0:T(8,128)(2,1)S(1)}, bf16[384,768]{1,0:T(8,128)(2,1)S(1)}, u32[]{:S(2)}, u32[]{:S(2)}) collective-permute-start(bf16[384,768]{1,0:T(8,128)(2,1)S(1)} %collective-permute-done.12), channel_id=1, source_target_pairs={{0,28},{4,0},{8,4},{12,8},{16,12},{20,16},{24,20},{28,24},{1,29},{... | collective-permute-start | bytes 1769480 | tf_op jit(solution)/shard_map/ppermute | solution.py:17
  150.7 34.4 %collective-permute-start.16 = (f32[1,384]{1,0:T(1,128)}, f32[1,384]{1,0:T(1,128)}, u32[]{:S(2)}, u32[]{:S(2)}) collective-permute-start(f32[1,384]{1,0:T(1,128)} %broadcast_in_dim.20), channel_id=1, source_target_pairs={{0,28},{4,0},{8,4},{12,8},{16,12},{20,16},{24,20},{28,24},{1,29},{... | collective-permute-start | bytes 4616 | tf_op jit(solution)/shard_map/ppermute | solution.py:17
  156.7 34.5 %collective-permute-start.20 = (f32[1,384]{1,0:T(1,128)}, f32[1,384]{1,0:T(1,128)}, u32[]{:S(2)}, u32[]{:S(2)}) collective-permute-start(f32[1,384]{1,0:T(1,128)} %broadcast_in_dim.24), channel_id=1, source_target_pairs={{0,4},{4,8},{8,12},{12,16},{16,20},{20,24},{24,28},{28,0},{1,5},{5... | collective-permute-start | bytes 4616 | tf_op jit(solution)/shard_map/ppermute | solution.py:17
  181.2 38.1 %copy-start.27 = (f32[64,384]{1,0:T(8,128)S(1)}, f32[64,384]{1,0:T(8,128)}, u32[]{:S(2)}) copy-start(f32[64,384]{1,0:T(8,128)} %param.7) | copy-start | bytes 294916
  185.1 95.2 %reduce-scatter.5.cloned.1.call-start = ((), (), s32[]{:S(2)}) async-start(), calls=%async_computation.3 | async-start | bytes 491520 | tf_op jit(solution)/shard_map/reduce_scatter | solution.py:58
  185.8 6.7 %collective-permute-start.17 = (f32[1,384]{1,0:T(1,128)S(1)}, f32[1,384]{1,0:T(1,128)S(1)}, u32[]{:S(2)}, u32[]{:S(2)}) collective-permute-start(f32[1,384]{1,0:T(1,128)S(1)} %reshape_add_fusion.5), channel_id=1, source_target_pairs={{0,28},{4,0},{8,4},{12,8},{16,12},{20,16},{24,20},{28,24},{1,29},{... | collective-permute-start | bytes 4616 | tf_op jit(solution)/shard_map/ppermute | solution.py:17
  191.9 4.5 %collective-permute-start.21 = (f32[1,384]{1,0:T(1,128)S(1)}, f32[1,384]{1,0:T(1,128)S(1)}, u32[]{:S(2)}, u32[]{:S(2)}) collective-permute-start(f32[1,384]{1,0:T(1,128)S(1)} %reshape_add_fusion.2), channel_id=1, source_target_pairs={{0,4},{4,8},{8,12},{12,16},{16,20},{20,24},{24,28},{28,0},{1,5},{5... | collective-permute-start | bytes 4616 | tf_op jit(solution)/shard_map/ppermute | solution.py:17
  192.5 4.5 %collective-permute-start.18 = (f32[1,384]{1,0:T(1,128)S(1)}, f32[1,384]{1,0:T(1,128)S(1)}, u32[]{:S(2)}, u32[]{:S(2)}) collective-permute-start(f32[1,384]{1,0:T(1,128)S(1)} %reshape_add_fusion.4), channel_id=1, source_target_pairs={{0,28},{4,0},{8,4},{12,8},{16,12},{20,16},{24,20},{28,24},{1,29},{... | collective-permute-start | bytes 4616 | tf_op jit(solution)/shard_map/ppermute | solution.py:17
  196.4 4.5 %collective-permute-start.22 = (f32[1,384]{1,0:T(1,128)S(1)}, f32[1,384]{1,0:T(1,128)S(1)}, u32[]{:S(2)}, u32[]{:S(2)}) collective-permute-start(f32[1,384]{1,0:T(1,128)S(1)} %reshape_add_fusion.1), channel_id=1, source_target_pairs={{0,4},{4,8},{8,12},{12,16},{16,20},{20,24},{24,28},{28,0},{1,5},{5... | collective-permute-start | bytes 4616 | tf_op jit(solution)/shard_map/ppermute | solution.py:17
  197.0 22.2 %collective-permute-start.19 = (f32[1,384]{1,0:T(1,128)S(1)}, f32[1,384]{1,0:T(1,128)S(1)}, u32[]{:S(2)}, u32[]{:S(2)}) collective-permute-start(f32[1,384]{1,0:T(1,128)S(1)} %reshape_add_fusion.3), channel_id=1, source_target_pairs={{0,28},{4,0},{8,4},{12,8},{16,12},{20,16},{24,20},{28,24},{1,29},{... | collective-permute-start | bytes 4616 | tf_op jit(solution)/shard_map/ppermute | solution.py:17
  200.9 18.4 %collective-permute-start.23 = (f32[1,384]{1,0:T(1,128)S(1)}, f32[1,384]{1,0:T(1,128)S(1)}, u32[]{:S(2)}, u32[]{:S(2)}) collective-permute-start(f32[1,384]{1,0:T(1,128)S(1)} %reshape_add_fusion), channel_id=1, source_target_pairs={{0,4},{4,8},{8,12},{12,16},{16,20},{20,24},{24,28},{28,0},{1,5},{5... | collective-permute-start | bytes 4616 | tf_op jit(solution)/shard_map/ppermute | solution.py:17
  225.0 9.4 %collective-permute-start.24 = (bf16[64,384]{1,0:T(8,128)(2,1)S(1)}, bf16[64,384]{1,0:T(8,128)(2,1)S(1)}, u32[]{:S(2)}, u32[]{:S(2)}) collective-permute-start(bf16[64,384]{1,0:T(8,128)(2,1)S(1)} %multiply_convert_fusion), channel_id=1, source_target_pairs={{0,4},{4,8},{8,12},{12,16},{16,20},{20,24},{24,28},{28,0},{1,5},{5... | collective-permute-start | bytes 147464 | tf_op jit(solution)/shard_map/ppermute | solution.py:17
  226.5 10.0 %collective-permute-start.28 = (bf16[64,384]{1,0:T(8,128)(2,1)S(1)}, bf16[64,384]{1,0:T(8,128)(2,1)S(1)}, u32[]{:S(2)}, u32[]{:S(2)}) collective-permute-start(bf16[64,384]{1,0:T(8,128)(2,1)S(1)} %multiply_convert_fusion), channel_id=1, source_target_pairs={{0,28},{4,0},{8,4},{12,8},{16,12},{20,16},{24,20},{28,24},{1,29},{... | collective-permute-start | bytes 147464 | tf_op jit(solution)/shard_map/ppermute | solution.py:17
  230.6 11.7 %collective-permute-start.32 = (f32[64,384]{1,0:T(8,128)S(1)}, f32[64,384]{1,0:T(8,128)S(1)}, u32[]{:S(2)}, u32[]{:S(2)}) collective-permute-start(f32[64,384]{1,0:T(8,128)S(1)} %fusion.18), channel_id=1, source_target_pairs={{0,28},{4,0},{8,4},{12,8},{16,12},{20,16},{24,20},{28,24},{1,29},{... | collective-permute-start | bytes 294920 | tf_op jit(solution)/shard_map/ppermute | solution.py:17
  232.4 20.6 %collective-permute-start.36 = (f32[64,384]{1,0:T(8,128)S(1)}, f32[64,384]{1,0:T(8,128)S(1)}, u32[]{:S(2)}, u32[]{:S(2)}) collective-permute-start(f32[64,384]{1,0:T(8,128)S(1)} %fusion.6), channel_id=1, source_target_pairs={{0,4},{4,8},{8,12},{12,16},{16,20},{20,24},{24,28},{28,0},{1,5},{5... | collective-permute-start | bytes 294920 | tf_op jit(solution)/shard_map/ppermute | solution.py:17
  234.5 5.3 %collective-permute-start.25 = (bf16[64,384]{1,0:T(8,128)(2,1)S(1)}, bf16[64,384]{1,0:T(8,128)(2,1)S(1)}, u32[]{:S(2)}, u32[]{:S(2)}) collective-permute-start(bf16[64,384]{1,0:T(8,128)(2,1)S(1)} %collective-permute-done.24), channel_id=1, source_target_pairs={{0,4},{4,8},{8,12},{12,16},{16,20},{20,24},{24,28},{28,0},{1,5},{5... | collective-permute-start | bytes 147464 | tf_op jit(solution)/shard_map/ppermute | solution.py:17
  236.5 5.1 %collective-permute-start.29 = (bf16[64,384]{1,0:T(8,128)(2,1)S(1)}, bf16[64,384]{1,0:T(8,128)(2,1)S(1)}, u32[]{:S(2)}, u32[]{:S(2)}) collective-permute-start(bf16[64,384]{1,0:T(8,128)(2,1)S(1)} %collective-permute-done.28), channel_id=1, source_target_pairs={{0,28},{4,0},{8,4},{12,8},{16,12},{20,16},{24,20},{28,24},{1,29},{... | collective-permute-start | bytes 147464 | tf_op jit(solution)/shard_map/ppermute | solution.py:17
  239.7 4.6 %collective-permute-start.26 = (bf16[64,384]{1,0:T(8,128)(2,1)S(1)}, bf16[64,384]{1,0:T(8,128)(2,1)S(1)}, u32[]{:S(2)}, u32[]{:S(2)}) collective-permute-start(bf16[64,384]{1,0:T(8,128)(2,1)S(1)} %collective-permute-done.25), channel_id=1, source_target_pairs={{0,4},{4,8},{8,12},{12,16},{16,20},{20,24},{24,28},{28,0},{1,5},{5... | collective-permute-start | bytes 147464 | tf_op jit(solution)/shard_map/ppermute | solution.py:17
  241.6 5.2 %collective-permute-start.30 = (bf16[64,384]{1,0:T(8,128)(2,1)S(1)}, bf16[64,384]{1,0:T(8,128)(2,1)S(1)}, u32[]{:S(2)}, u32[]{:S(2)}) collective-permute-start(bf16[64,384]{1,0:T(8,128)(2,1)S(1)} %collective-permute-done.29), channel_id=1, source_target_pairs={{0,28},{4,0},{8,4},{12,8},{16,12},{20,16},{24,20},{28,24},{1,29},{... | collective-permute-start | bytes 147464 | tf_op jit(solution)/shard_map/ppermute | solution.py:17
  242.6 14.6 %collective-permute-start.33 = (f32[64,384]{1,0:T(8,128)S(1)}, f32[64,384]{1,0:T(8,128)S(1)}, u32[]{:S(2)}, u32[]{:S(2)}) collective-permute-start(f32[64,384]{1,0:T(8,128)S(1)} %convolution_add_fusion.8), channel_id=1, source_target_pairs={{0,28},{4,0},{8,4},{12,8},{16,12},{20,16},{24,20},{28,24},{1,29},{... | collective-permute-start | bytes 294920 | tf_op jit(solution)/shard_map/ppermute | solution.py:17
  244.3 5.0 %collective-permute-start.27 = (bf16[64,384]{1,0:T(8,128)(2,1)S(1)}, bf16[64,384]{1,0:T(8,128)(2,1)S(1)}, u32[]{:S(2)}, u32[]{:S(2)}) collective-permute-start(bf16[64,384]{1,0:T(8,128)(2,1)S(1)} %collective-permute-done.26), channel_id=1, source_target_pairs={{0,4},{4,8},{8,12},{12,16},{16,20},{20,24},{24,28},{28,0},{1,5},{5... | collective-permute-start | bytes 147464 | tf_op jit(solution)/shard_map/ppermute | solution.py:17
  246.8 5.0 %collective-permute-start.31 = (bf16[64,384]{1,0:T(8,128)(2,1)S(1)}, bf16[64,384]{1,0:T(8,128)(2,1)S(1)}, u32[]{:S(2)}, u32[]{:S(2)}) collective-permute-start(bf16[64,384]{1,0:T(8,128)(2,1)S(1)} %collective-permute-done.30), channel_id=1, source_target_pairs={{0,28},{4,0},{8,4},{12,8},{16,12},{20,16},{24,20},{28,24},{1,29},{... | collective-permute-start | bytes 147464 | tf_op jit(solution)/shard_map/ppermute | solution.py:17
  254.7 6.5 %collective-permute-start.37 = (f32[64,384]{1,0:T(8,128)S(1)}, f32[64,384]{1,0:T(8,128)S(1)}, u32[]{:S(2)}, u32[]{:S(2)}) collective-permute-start(f32[64,384]{1,0:T(8,128)S(1)} %convolution_add_fusion.7), channel_id=1, source_target_pairs={{0,4},{4,8},{8,12},{12,16},{16,20},{20,24},{24,28},{28,0},{1,5},{5... | collective-permute-start | bytes 294920 | tf_op jit(solution)/shard_map/ppermute | solution.py:17
  257.2 7.1 %collective-permute-start.34 = (f32[64,384]{1,0:T(8,128)S(1)}, f32[64,384]{1,0:T(8,128)S(1)}, u32[]{:S(2)}, u32[]{:S(2)}) collective-permute-start(f32[64,384]{1,0:T(8,128)S(1)} %add.429), channel_id=1, source_target_pairs={{0,28},{4,0},{8,4},{12,8},{16,12},{20,16},{24,20},{28,24},{1,29},{... | collective-permute-start | bytes 294920 | tf_op jit(solution)/shard_map/ppermute | solution.py:17
  261.2 6.4 %collective-permute-start.38 = (f32[64,384]{1,0:T(8,128)S(1)}, f32[64,384]{1,0:T(8,128)S(1)}, u32[]{:S(2)}, u32[]{:S(2)}) collective-permute-start(f32[64,384]{1,0:T(8,128)S(1)} %add.433), channel_id=1, source_target_pairs={{0,4},{4,8},{8,12},{12,16},{16,20},{20,24},{24,28},{28,0},{1,5},{5... | collective-permute-start | bytes 294920 | tf_op jit(solution)/shard_map/ppermute | solution.py:17
  264.3 7.6 %collective-permute-start.35 = (f32[64,384]{1,0:T(8,128)S(1)}, f32[64,384]{1,0:T(8,128)S(1)}, u32[]{:S(2)}, u32[]{:S(2)}) collective-permute-start(f32[64,384]{1,0:T(8,128)S(1)} %add.430), channel_id=1, source_target_pairs={{0,28},{4,0},{8,4},{12,8},{16,12},{20,16},{24,20},{28,24},{1,29},{... | collective-permute-start | bytes 294920 | tf_op jit(solution)/shard_map/ppermute | solution.py:17
  267.7 5.3 %collective-permute-start.39 = (f32[64,384]{1,0:T(8,128)S(1)}, f32[64,384]{1,0:T(8,128)S(1)}, u32[]{:S(2)}, u32[]{:S(2)}) collective-permute-start(f32[64,384]{1,0:T(8,128)S(1)} %add.434), channel_id=1, source_target_pairs={{0,4},{4,8},{8,12},{12,16},{16,20},{20,24},{24,28},{28,0},{1,5},{5... | collective-permute-start | bytes 294920 | tf_op jit(solution)/shard_map/ppermute | solution.py:17
  (44 other events, 280.3 us)
Sparse Core Ops, SparseCore 0:
  8.9 25.1 all-gather.1
  185.2 32.9 reduce-scatter.6
  253.1 27.1 reduce-scatter.4
